TPU v7x, 128 devices: a whole 4x4x4 slice. The times are simulated.
128 devices in a mesh: gx: 16 (over z, y), gy: 8 (over x, core).
Axes of the slice: x: 4, y: 4, z: 4, core: 2. Of those that a mesh axis runs over, the one named last changes fastest.
Arguments:
- centers: float32 [3, 262144], P(None, ('gx', 'gy')), may hold values from -6 to 6
- tilt_angle: float32 [262144], P(('gx', 'gy')), may hold values from -3.140625 to 3.140625
- turn_angle: float32 [262144], P(('gx', 'gy')), may hold values from -3.140625 to 3.140625
- radius: float32 [262144], P(('gx', 'gy')), may hold values from 0.5 to 2
- mobility_perp: float32 [262144], P(('gx', 'gy')), may hold values from 0.3 to 3
- mobility_axial: float32 [262144], P(('gx', 'gy')), may hold values from 0.2 to 2
- mobility_rot: float32 [262144], P(('gx', 'gy')), may hold values from 0.3 to 3
- external_load: float32 [6, 262144], P(None, ('gx', 'gy')), may hold values from -60 to 60
- local_first: int32 [327680], P(('gx', 'gy')), may hold values from 0 to 2047, as said below
- local_second: int32 [327680], P(('gx', 'gy')), may hold values from 0 to 2047
- arc_first: float32 [327680], P(('gx', 'gy')), may hold values from -1 to 1
- arc_second: float32 [327680], P(('gx', 'gy')), may hold values from -1 to 1
- cross_mine: int32 [128, 4, 256], P(('gx', 'gy')), may hold values from 0 to 2047
- cross_slot: int32 [128, 4, 256], P(('gx', 'gy')), may hold values from 0 to 127
- cross_arc_own: float32 [128, 4, 256], P(('gx', 'gy')), may hold values from -1 to 1
- cross_arc_other: float32 [128, 4, 256], P(('gx', 'gy')), may hold values from -1 to 1
- cross_count: int32 [128, 4], P(('gx', 'gy')), may hold values from 0 to 256, as said below
- export_rows: int32 [128, 4, 128], P(('gx', 'gy')), may hold values from 0 to 2047
Outputs:
- velocity: float32 [6, 262144], P(None, ('gx', 'gy'))
- force_local: float32 [327680], P(('gx', 'gy'))
- force_cross: float32 [128, 4, 256], P(('gx', 'gy'))
Inputs may be any that keep to these rules, and one draw needn't show every extreme that they name: local_second never equals local_first of the same pair. Slots c < cross_count[k, d] are live, the others dead. A direction whose partner lies outside the mesh has count 0. In every draw some block holds 256 live pairs.
All inputs are finite; a program needn't handle non-finite values.
Results may differ from a plain program's by a relative error of at most 0.00002.
Values sent between devices are 32-bit elements; how exact they have to be, the bound alone decides.
A program may use at most 64 MiB of HBM per device.

v0:
```python
import jax
import jax.numpy as jnp
from jax import lax
from jax.sharding import PartitionSpec as P

step_time = 0.5
floor_gap = 0.25
tiny = 1e-06


def passed_along(shard, axis, by):
    devices = lax.axis_size(axis)
    pairs = [(i, i + by) for i in range(devices) if 0 <= i + by < devices]
    return lax.ppermute(shard, axis, pairs)


def tangent_of(polar, azimuth):
    lifted = jnp.sin(polar)
    return jnp.stack([lifted * jnp.cos(azimuth), lifted * jnp.sin(azimuth), jnp.cos(polar)])


def cross_product(left, right):
    return jnp.stack(
        [
            left[1] * right[2] - left[2] * right[1],
            left[2] * right[0] - left[0] * right[2],
            left[0] * right[1] - left[1] * right[0],
        ]
    )


def pair_terms(geo_first, geo_second, arc_one, arc_two, live_mask):
    lever_first = arc_one * tangent_of(geo_first[3], geo_first[4])
    lever_second = arc_two * tangent_of(geo_second[3], geo_second[4])
    apart = geo_first[:3] + lever_first - geo_second[:3] - lever_second
    spacing = jnp.sqrt(jnp.sum(apart * apart, axis=0))
    normal = apart / jnp.maximum(spacing, floor_gap) * live_mask
    jacobian = jnp.concatenate(
        [normal, cross_product(lever_first, normal), cross_product(lever_second, normal)], axis=0
    )
    clearance = (spacing - geo_first[5] - geo_second[5]) * live_mask
    return (jacobian, clearance)


def rate_of(jacobian, moving_first, moving_second):
    return (
        jnp.sum(jacobian[:3] * (moving_first[:3] - moving_second[:3]), axis=0)
        + jnp.sum(jacobian[3:6] * moving_first[3:], axis=0)
        - jnp.sum(jacobian[6:] * moving_second[3:], axis=0)
    )


def push_terms(jacobian, amount):
    return (amount * jacobian[:6], -amount * jnp.concatenate([jacobian[:3], jacobian[6:]], axis=0))


def apply_mobility(applied, tangent, perp, axial, rotary):
    force = applied[:3]
    along = jnp.sum(tangent * force, axis=0)
    return jnp.concatenate([perp * force + axial * along * tangent, rotary * applied[3:]], axis=0)


def toward_owner(blocks):
    across = lax.axis_size("gy")
    received = []
    for position, offset in enumerate((1, across + 1, across, across - 1)):
        received.append(passed_along(blocks[position], ("gx", "gy"), -offset))
    return jnp.stack(received)


def toward_partner(blocks):
    across = lax.axis_size("gy")
    received = []
    for position, offset in enumerate((1, across + 1, across, across - 1)):
        received.append(passed_along(blocks[position], ("gx", "gy"), offset))
    return jnp.stack(received)


def sum_pairs(first_term, second_term):
    return lax.psum((first_term, second_term), ("gx", "gy"))


def on_device(
    centers,
    tilt_angle,
    turn_angle,
    radius,
    mobility_perp,
    mobility_axial,
    mobility_rot,
    external_load,
    local_first,
    local_second,
    arc_first,
    arc_second,
    cross_mine,
    cross_slot,
    cross_arc_own,
    cross_arc_other,
    cross_count,
    export_rows,
):
    seg_rows = centers.shape[1]
    local_pairs = local_first.shape[0]
    blocks_cap = cross_mine.shape[2]
    export_cap = export_rows.shape[2]
    geometry = jnp.concatenate([centers, tilt_angle[None], turn_angle[None], radius[None]], axis=0)
    tangent = tangent_of(tilt_angle, turn_angle)
    exported = export_rows[0]
    export_flat = exported.reshape(-1)
    own_rows = cross_mine[0].reshape(-1)
    all_rows = jnp.concatenate([local_first, local_second, own_rows])
    slot_flat = (cross_slot[0] + (jnp.arange(4, dtype=jnp.int32) * export_cap)[:, None]).reshape(-1)
    live_mask = (
        (jnp.arange(blocks_cap, dtype=jnp.int32)[None, :] < cross_count[0][:, None])
        .astype(jnp.float32)
        .reshape(-1)
    )

    def picked(source):
        taken = jnp.take(source, all_rows, axis=1)
        return (
            taken[:, :local_pairs],
            taken[:, local_pairs : 2 * local_pairs],
            taken[:, 2 * local_pairs :],
        )

    def outgoing(source):
        return jnp.moveaxis(jnp.take(source, exported, axis=1), 1, 0)

    def incoming(blocks):
        flattened = jnp.moveaxis(blocks, 0, 1).reshape(blocks.shape[1], -1)
        return jnp.take(flattened, slot_flat, axis=1)

    def mobile(applied):
        return apply_mobility(applied, tangent, mobility_perp, mobility_axial, mobility_rot)

    drift = mobile(external_load)
    remote_geometry = incoming(toward_owner(outgoing(geometry)))
    geo_one, geo_two, geo_own = picked(geometry)
    jacobian_local, clearance_local = pair_terms(geo_one, geo_two, arc_first, arc_second, 1.0)
    jacobian_cross, clearance_cross = pair_terms(
        geo_own,
        remote_geometry,
        cross_arc_own[0].reshape(-1),
        cross_arc_other[0].reshape(-1),
        live_mask,
    )

    def spread(amount_local, amount_cross):
        local_one, local_two = push_terms(jacobian_local, amount_local)
        cross_one, cross_two = push_terms(jacobian_cross, amount_cross)
        slot_loads = jnp.zeros((6, 4 * export_cap), jnp.float32).at[:, slot_flat].add(cross_two)
        returned = toward_partner(jnp.moveaxis(slot_loads.reshape(6, 4, export_cap), 1, 0))
        pushes = jnp.concatenate([local_one, local_two, cross_one], axis=1)
        loads = jnp.zeros((6, seg_rows), jnp.float32).at[:, all_rows].add(pushes)
        return loads.at[:, export_flat].add(jnp.moveaxis(returned, 0, 1).reshape(6, -1))

    def rates(moving, remote_moving=None):
        remote_moving = incoming(toward_owner(outgoing(moving)))
        move_one, move_two, move_own = picked(moving)
        rate_local = rate_of(jacobian_local, move_one, move_two)
        rate_cross = rate_of(jacobian_cross, move_own, remote_moving)
        return (rate_local, rate_cross)

    drift_local, drift_cross = rates(drift, None)
    slope_local = clearance_local / step_time + drift_local
    slope_cross = clearance_cross / step_time + drift_cross
    top_first = jnp.sum(slope_local * slope_local) + jnp.sum(slope_cross * slope_cross)
    loads_first = spread(slope_local, slope_cross)
    moved_first = mobile(loads_first)
    curved_local, curved_cross = rates(moved_first)
    top_first, bottom_first = sum_pairs(
        top_first, jnp.sum(slope_local * curved_local) + jnp.sum(slope_cross * curved_cross)
    )
    step_first = top_first / (bottom_first + tiny)
    thrust_local = jnp.maximum(0.0, -step_first * slope_local)
    thrust_cross = jnp.maximum(0.0, -step_first * slope_cross)
    loads_second = spread(thrust_local, thrust_cross)
    moved_second = mobile(loads_second)
    moving_one = drift + moved_second
    top_second = jnp.sum(thrust_local * thrust_local) + jnp.sum(thrust_cross * thrust_cross)
    rate_local, rate_cross = rates(moving_one)
    next_local = clearance_local / step_time + rate_local
    next_cross = clearance_cross / step_time + rate_cross
    top_second, bottom_second = sum_pairs(
        top_second,
        jnp.sum(thrust_local * (next_local - slope_local))
        + jnp.sum(thrust_cross * (next_cross - slope_cross)),
    )
    step_second = top_second / (bottom_second + tiny)
    force_local = jnp.maximum(0.0, thrust_local - step_second * next_local)
    force_cross = jnp.maximum(0.0, thrust_cross - step_second * next_cross)
    velocity = drift + mobile(spread(force_local, force_cross))
    return (velocity, force_local, force_cross.reshape(1, 4, blocks_cap))


def solution(mesh):
    return jax.shard_map(
        on_device,
        mesh=mesh,
        in_specs=(
            P(None, ("gx", "gy")),
            P(("gx", "gy")),
            P(("gx", "gy")),
            P(("gx", "gy")),
            P(("gx", "gy")),
            P(("gx", "gy")),
            P(("gx", "gy")),
            P(None, ("gx", "gy")),
            P(("gx", "gy")),
            P(("gx", "gy")),
            P(("gx", "gy")),
            P(("gx", "gy")),
            P(("gx", "gy"), None, None),
            P(("gx", "gy"), None, None),
            P(("gx", "gy"), None, None),
            P(("gx", "gy"), None, None),
            P(("gx", "gy"), None),
            P(("gx", "gy"), None, None),
        ),
        out_specs=(P(None, ("gx", "gy")), P(("gx", "gy")), P(("gx", "gy"), None, None)),
        check_vma=False,
    )
```

profile of v0, /device:TPU:1, one launch (start us, length us, event | category | flops | bytes accessed | tf_op | source)
XLA Modules:
  0.0 529.1 jit_solution(2936644011537897512)
XLA Ops:
  11.4 3.3 collective-permute-start
  14.7 1.3 collective-permute-start.1
  16.0 1.3 collective-permute-start.2
  17.3 1.3 collective-permute-start.3
  19.2 1.9 collective-permute-start.4
  23.0 20.9 %gather_fusion.1 = f32[6144,6]{1,0:T(8,128)} fusion(f32[6,2048]{0,1:T(8,128)S(1)} %copy.319, s32[6144]{0:T(1024)S(1)} %fusion.33), kind=kCustom, calls=%fused_computation.3.clone | custom fusion | bytes 319488 | tf_op jit(solution)/shard_map/jit(_take)/gather | solution.py:121
  43.9 20.9 %gather_fusion = f32[6144,6]{1,0:T(8,128)} fusion(f32[6,2048]{0,1:T(8,128)S(1)} %copy.317, s32[6144]{0:T(1024)S(1)} %fusion.33), kind=kCustom, calls=%fused_computation.clone | custom fusion | bytes 319488 | tf_op jit(solution)/shard_map/jit(_take)/gather | solution.py:121
  66.0 2.4 copy.320
  72.4 1.9 slice_reduce_fusion.1
  75.3 1.3 reshape_dynamic-update-slice_fusion
  88.5 3.3 gather_fusion.3
  92.7 1.6 collective-permute-done.7
  94.6 2.8 gather_fusion.5
  100.2 6.1 %scatter_custom_fusion.1 = f32[6,512]{0,1:T(8,128)S(1)} fusion(s32[1024]{0:T(1024)S(1)} %bitcast.296, f32[1024,6]{1,0:T(8,128)S(1)} %copy.336, f32[]{:T(128)} %constant.32.clone.1), kind=kCustom, calls=%fused_computation.39 | custom fusion | flops 6144 | bytes 12292 | tf_op jit(solution)/shard_map/scatter-add | solution.py:153
  106.4 4.1 collective-permute-start.8
  110.4 5.0 collective-permute-start.9
  115.5 5.1 collective-permute-start.10
  120.6 6.2 %collective-permute-start.11 = (f32[6,128]{1,0:T(8,128)S(1)}, f32[6,128]{1,0:T(8,128)S(1)}, u32[]{:S(2)}, u32[]{:S(2)}) collective-permute-start(f32[6,128]{1,0:T(8,128)S(1)} %get-tuple-element.130), channel_id=1, source_target_pairs={{0,7},{1,8},{2,9},{3,10},{4,11},{5,12},{6,13},{7,14},{8,15},{9,16}... | collective-permute-start | bytes 9224 | tf_op jit(solution)/shard_map/ppermute | solution.py:14
  128.0 2.2 copy.335
  130.8 33.7 %scatter_custom_fusion = f32[6,2048]{0,1:T(8,128)S(1)} fusion(s32[6144]{0:T(1024)S(1)} %bitcast.275, f32[6144,6]{1,0:T(8,128)} %copy.335, f32[]{:T(128)} %constant.32.clone.1), kind=kCustom, calls=%fused_computation.25 | custom fusion | flops 36864 | bytes 49664 | tf_op jit(solution)/shard_map/scatter-add | solution.py:156
  164.9 4.2 scatter_fusion
  171.8 20.9 %gather_fusion.6 = f32[6144,6]{1,0:T(8,128)} fusion(f32[6,2048]{0,1:T(8,128)S(1)} %copy.344, s32[6144]{0:T(1024)S(1)} %copy-done.4), kind=kCustom, calls=%fused_computation.4.clone | custom fusion | bytes 319488 | tf_op jit(solution)/shard_map/jit(_take)/gather | solution.py:121
  192.9 3.2 collective-permute-start.12
  200.0 2.4 copy.345
  204.3 4.1 collective-permute-done.15
  208.6 2.8 gather_fusion.8
  215.5 74.8 %all-reduce.1 = (f32[]{:T(128)}, f32[]{:T(128)}) all-reduce(f32[]{:T(128)S(6)} %add.310, f32[]{:T(128)S(6)} %add.319), channel_id=1, replica_groups=mesh['gx'=16,'gy'=8] {'gx','gy'}, use_global_device_ids=true, to_apply=%region_11.15 | all-reduce | flops 2 | bytes 16 | tf_op jit(solution)/shard_map/psum | solution.py:80
  291.9 6.2 %scatter_custom_fusion.4 = f32[6,512]{0,1:T(8,128)S(1)} fusion(s32[1024]{0:T(1024)} %bitcast.297, f32[1024,6]{1,0:T(8,128)S(1)} %copy.354, f32[]{:T(128)} %constant.32.clone.1), kind=kCustom, calls=%fused_computation.37 | custom fusion | flops 6144 | bytes 12800 | tf_op jit(solution)/shard_map/scatter-add | solution.py:153
  298.2 3.8 collective-permute-start.16
  303.4 3.1 collective-permute-start.18
  306.5 2.8 collective-permute-start.19
  309.6 2.2 copy.353
  311.8 33.7 %scatter_custom_fusion.3 = f32[6,2048]{0,1:T(8,128)S(1)} fusion(s32[6144]{0:T(1024)} %bitcast.276, f32[6144,6]{1,0:T(8,128)} %copy.353, f32[]{:T(128)} %constant.32.clone.1), kind=kCustom, calls=%fused_computation.23 | custom fusion | flops 36864 | bytes 49664 | tf_op jit(solution)/shard_map/scatter-add | solution.py:156
  345.8 3.9 scatter_fusion.1
  351.4 20.9 %gather_fusion.9 = f32[6144,6]{1,0:T(8,128)} fusion(f32[6,2048]{0,1:T(8,128)S(1)} %copy.362, s32[6144]{0:T(1024)S(1)} %copy-done.4), kind=kCustom, calls=%fused_computation.5.clone | custom fusion | bytes 319488 | tf_op jit(solution)/shard_map/jit(_take)/gather | solution.py:121
  373.6 2.4 copy.363
  376.3 4.9 collective-permute-start.20
  387.1 3.7 collective-permute-done.23
  391.0 2.8 gather_fusion.11
  397.4 68.4 %all-reduce = (f32[]{:T(128)}, f32[]{:T(128)}) all-reduce(f32[]{:T(128)S(6)} %add.321, f32[]{:T(128)S(6)} %add.328), channel_id=1, replica_groups=mesh['gx'=16,'gy'=8] {'gx','gy'}, use_global_device_ids=true, to_apply=%region_27.31 | all-reduce | flops 2 | bytes 16 | tf_op jit(solution)/shard_map/psum | solution.py:80
  468.0 6.2 %scatter_custom_fusion.7 = f32[6,512]{0,1:T(8,128)S(1)} fusion(s32[1024]{0:T(1024)} %bitcast.298, f32[1024,6]{1,0:T(8,128)S(1)} %copy.372, f32[]{:T(128)} %constant.32.clone.1), kind=kCustom, calls=%fused_computation.35 | custom fusion | flops 6144 | bytes 12800 | tf_op jit(solution)/shard_map/scatter-add | solution.py:153
  474.4 1.9 collective-permute-start.24
  476.3 2.4 collective-permute-start.25
  478.7 2.2 collective-permute-start.26
  480.9 5.0 collective-permute-start.27
  486.9 2.2 copy.371
  489.1 33.7 %scatter_custom_fusion.6 = f32[6,2048]{0,1:T(8,128)S(1)} fusion(s32[6144]{0:T(1024)} %bitcast.277, f32[6144,6]{1,0:T(8,128)} %copy.371, f32[]{:T(128)} %constant.32.clone.1), kind=kCustom, calls=%fused_computation.21 | custom fusion | flops 36864 | bytes 49664 | tf_op jit(solution)/shard_map/scatter-add | solution.py:156
  523.1 3.9 scatter_fusion.2
  (379 shorter events, 62.8 us)
Async XLA Ops:
  2.1 62.7 %copy-start.73 = (pred[4,128]{1,0:T(4,128)(4,1)}, pred[4,128]{1,0:T(4,128)(4,1)S(1)}, u32[]{:S(2)}) copy-start(pred[4,128]{1,0:T(4,128)(4,1)S(1)} %compare_and_fusion.2) | copy-start | bytes 1540
  7.2 58.2 %copy-start.56 = (s32[1024]{0:T(1024)}, s32[1024]{0:T(1024)S(1)}, u32[]{:S(2)}) copy-start(s32[1024]{0:T(1024)S(1)} %pad_clamp_fusion) | copy-start | bytes 12292
  11.4 70.4 %collective-permute-start = (f32[6,128]{1,0:T(8,128)}, f32[6,128]{1,0:T(8,128)}, u32[]{:S(2)}, u32[]{:S(2)}) collective-permute-start(f32[6,128]{1,0:T(8,128)} %get-tuple-element.141), channel_id=1, source_target_pairs={{1,0},{2,1},{3,2},{4,3},{5,4},{6,5},{7,6},{8,7},{9,8},{10,9},{11,1... | collective-permute-start | bytes 9224 | tf_op jit(solution)/shard_map/ppermute | solution.py:14
  14.7 69.1 %collective-permute-start.1 = (f32[6,128]{1,0:T(8,128)}, f32[6,128]{1,0:T(8,128)}, u32[]{:S(2)}, u32[]{:S(2)}) collective-permute-start(f32[6,128]{1,0:T(8,128)} %get-tuple-element.144), channel_id=1, source_target_pairs={{9,0},{10,1},{11,2},{12,3},{13,4},{14,5},{15,6},{16,7},{17,8},{18,... | collective-permute-start | bytes 9224 | tf_op jit(solution)/shard_map/ppermute | solution.py:14
  16.0 69.7 %collective-permute-start.2 = (f32[6,128]{1,0:T(8,128)}, f32[6,128]{1,0:T(8,128)}, u32[]{:S(2)}, u32[]{:S(2)}) collective-permute-start(f32[6,128]{1,0:T(8,128)} %get-tuple-element.143), channel_id=1, source_target_pairs={{8,0},{9,1},{10,2},{11,3},{12,4},{13,5},{14,6},{15,7},{16,8},{17,9... | collective-permute-start | bytes 9224 | tf_op jit(solution)/shard_map/ppermute | solution.py:14
  17.3 70.4 %collective-permute-start.3 = (f32[6,128]{1,0:T(8,128)}, f32[6,128]{1,0:T(8,128)}, u32[]{:S(2)}, u32[]{:S(2)}) collective-permute-start(f32[6,128]{1,0:T(8,128)} %get-tuple-element.142), channel_id=1, source_target_pairs={{7,0},{8,1},{9,2},{10,3},{11,4},{12,5},{13,6},{14,7},{15,8},{16,9}... | collective-permute-start | bytes 9224 | tf_op jit(solution)/shard_map/ppermute | solution.py:14
  19.2 72.9 %collective-permute-start.4 = (f32[6,128]{1,0:T(8,128)}, f32[6,128]{1,0:T(8,128)}, u32[]{:S(2)}, u32[]{:S(2)}) collective-permute-start(f32[6,128]{1,0:T(8,128)} %get-tuple-element.137), channel_id=1, source_target_pairs={{1,0},{2,1},{3,2},{4,3},{5,4},{6,5},{7,6},{8,7},{9,8},{10,9},{11,1... | collective-permute-start | bytes 9224 | tf_op jit(solution)/shard_map/ppermute | solution.py:14
  78.7 52.1 %copy-start.61 = (s32[6144,1]{0,1:T(1,128)}, s32[6144,1]{0,1:T(1,128)S(1)}, u32[]{:S(2)}) copy-start(s32[6144,1]{0,1:T(1,128)S(1)} %compare_select_fusion) | copy-start | bytes 73732
  78.7 51.5 %copy-start.76 = (s32[1024,1]{0,1:T(1,128)}, s32[1024,1]{0,1:T(1,128)S(1)}, u32[]{:S(2)}) copy-start(s32[1024,1]{0,1:T(1,128)S(1)} %compare_select_fusion.2) | copy-start | bytes 12292
  80.3 84.6 %copy-start.58 = (s32[512,1]{0,1:T(1,128)}, s32[512,1]{0,1:T(1,128)S(1)}, u32[]{:S(2)}) copy-start(s32[512,1]{0,1:T(1,128)S(1)} %compare_select_fusion.3) | copy-start | bytes 6148
  81.7 48.5 %copy-start.38 = (f32[1,2,4,128]{3,1,2,0:T(2,128)}, f32[1,2,4,128]{3,1,2,0:T(2,128)S(1)}, u32[]{:S(2)}) copy-start(f32[1,2,4,128]{3,1,2,0:T(2,128)S(1)} %copy.396) | copy-start | bytes 12292
  81.7 11.0 %collective-permute-start.5 = (f32[6,128]{1,0:T(8,128)}, f32[6,128]{1,0:T(8,128)S(1)}, u32[]{:S(2)}, u32[]{:S(2)}) collective-permute-start(f32[6,128]{1,0:T(8,128)} %get-tuple-element.140), channel_id=1, source_target_pairs={{9,0},{10,1},{11,2},{12,3},{13,4},{14,5},{15,6},{16,7},{17,8},{18,... | collective-permute-start | bytes 9224 | tf_op jit(solution)/shard_map/ppermute | solution.py:14
  83.7 9.0 %collective-permute-start.6 = (f32[6,128]{1,0:T(8,128)}, f32[6,128]{1,0:T(8,128)S(1)}, u32[]{:S(2)}, u32[]{:S(2)}) collective-permute-start(f32[6,128]{1,0:T(8,128)} %get-tuple-element.139), channel_id=1, source_target_pairs={{8,0},{9,1},{10,2},{11,3},{12,4},{13,5},{14,6},{15,7},{16,8},{17,9... | collective-permute-start | bytes 9224 | tf_op jit(solution)/shard_map/ppermute | solution.py:14
  85.7 8.7 %collective-permute-start.7 = (f32[6,128]{1,0:T(8,128)}, f32[6,128]{1,0:T(8,128)S(1)}, u32[]{:S(2)}, u32[]{:S(2)}) collective-permute-start(f32[6,128]{1,0:T(8,128)} %get-tuple-element.138), channel_id=1, source_target_pairs={{7,0},{8,1},{9,2},{10,3},{11,4},{12,5},{13,6},{14,7},{15,8},{16,9}... | collective-permute-start | bytes 9224 | tf_op jit(solution)/shard_map/ppermute | solution.py:14
  98.8 65.8 %copy-start.9 = (f32[1,1024]{1,0:T(1,128)}, f32[1,1024]{1,0:T(1,128)S(1)}, u32[]{:S(2)}) copy-start(f32[1,1024]{1,0:T(1,128)S(1)} %get-tuple-element.106) | copy-start | bytes 12292
  98.8 65.8 %copy-start.12 = (f32[1,1024]{1,0:T(1,128)}, f32[1,1024]{1,0:T(1,128)S(1)}, u32[]{:S(2)}) copy-start(f32[1,1024]{1,0:T(1,128)S(1)} %get-tuple-element.107) | copy-start | bytes 12292
  98.8 65.8 %copy-start.15 = (f32[1,1024]{1,0:T(1,128)}, f32[1,1024]{1,0:T(1,128)S(1)}, u32[]{:S(2)}) copy-start(f32[1,1024]{1,0:T(1,128)S(1)} %get-tuple-element.108) | copy-start | bytes 12292
  106.4 58.2 %collective-permute-start.8 = (f32[6,128]{1,0:T(8,128)S(1)}, f32[6,128]{1,0:T(8,128)S(1)}, u32[]{:S(2)}, u32[]{:S(2)}) collective-permute-start(f32[6,128]{1,0:T(8,128)S(1)} %get-tuple-element.129), channel_id=1, source_target_pairs={{0,1},{1,2},{2,3},{3,4},{4,5},{5,6},{6,7},{7,8},{8,9},{9,10},{10,1... | collective-permute-start | bytes 9224 | tf_op jit(solution)/shard_map/ppermute | solution.py:14
  110.4 54.2 %collective-permute-start.9 = (f32[6,128]{1,0:T(8,128)S(1)}, f32[6,128]{1,0:T(8,128)S(1)}, u32[]{:S(2)}, u32[]{:S(2)}) collective-permute-start(f32[6,128]{1,0:T(8,128)S(1)} %get-tuple-element.132), channel_id=1, source_target_pairs={{0,9},{1,10},{2,11},{3,12},{4,13},{5,14},{6,15},{7,16},{8,17},{9,1... | collective-permute-start | bytes 9224 | tf_op jit(solution)/shard_map/ppermute | solution.py:14
  115.5 49.2 %collective-permute-start.10 = (f32[6,128]{1,0:T(8,128)S(1)}, f32[6,128]{1,0:T(8,128)S(1)}, u32[]{:S(2)}, u32[]{:S(2)}) collective-permute-start(f32[6,128]{1,0:T(8,128)S(1)} %get-tuple-element.131), channel_id=1, source_target_pairs={{0,8},{1,9},{2,10},{3,11},{4,12},{5,13},{6,14},{7,15},{8,16},{9,17... | collective-permute-start | bytes 9224 | tf_op jit(solution)/shard_map/ppermute | solution.py:14
  120.6 44.1 %collective-permute-start.11 = (f32[6,128]{1,0:T(8,128)S(1)}, f32[6,128]{1,0:T(8,128)S(1)}, u32[]{:S(2)}, u32[]{:S(2)}) collective-permute-start(f32[6,128]{1,0:T(8,128)S(1)} %get-tuple-element.130), channel_id=1, source_target_pairs={{0,7},{1,8},{2,9},{3,10},{4,11},{5,12},{6,13},{7,14},{8,15},{9,16}... | collective-permute-start | bytes 9224 | tf_op jit(solution)/shard_map/ppermute | solution.py:14
  192.9 11.0 %collective-permute-start.12 = (f32[6,128]{1,0:T(8,128)S(1)}, f32[6,128]{1,0:T(8,128)S(1)}, u32[]{:S(2)}, u32[]{:S(2)}) collective-permute-start(f32[6,128]{1,0:T(8,128)S(1)} %get-tuple-element.125), channel_id=1, source_target_pairs={{1,0},{2,1},{3,2},{4,3},{5,4},{6,5},{7,6},{8,7},{9,8},{10,9},{11,1... | collective-permute-start | bytes 9224 | tf_op jit(solution)/shard_map/ppermute | solution.py:14
  196.1 7.8 %collective-permute-start.13 = (f32[6,128]{1,0:T(8,128)S(1)}, f32[6,128]{1,0:T(8,128)S(1)}, u32[]{:S(2)}, u32[]{:S(2)}) collective-permute-start(f32[6,128]{1,0:T(8,128)S(1)} %get-tuple-element.128), channel_id=1, source_target_pairs={{9,0},{10,1},{11,2},{12,3},{13,4},{14,5},{15,6},{16,7},{17,8},{18,... | collective-permute-start | bytes 9224 | tf_op jit(solution)/shard_map/ppermute | solution.py:14
  197.4 6.9 %collective-permute-start.14 = (f32[6,128]{1,0:T(8,128)S(1)}, f32[6,128]{1,0:T(8,128)S(1)}, u32[]{:S(2)}, u32[]{:S(2)}) collective-permute-start(f32[6,128]{1,0:T(8,128)S(1)} %get-tuple-element.127), channel_id=1, source_target_pairs={{8,0},{9,1},{10,2},{11,3},{12,4},{13,5},{14,6},{15,7},{16,8},{17,9... | collective-permute-start | bytes 9224 | tf_op jit(solution)/shard_map/ppermute | solution.py:14
  198.7 110.7 %copy-start.49 = (f32[1,2560]{1,0:T(1,128)S(1)}, f32[1,2560]{1,0:T(1,128)}, u32[]{:S(2)}) copy-start(f32[1,2560]{1,0:T(1,128)} %get-tuple-element.61) | copy-start | bytes 30724
  198.7 9.7 %collective-permute-start.15 = (f32[6,128]{1,0:T(8,128)S(1)}, f32[6,128]{1,0:T(8,128)S(1)}, u32[]{:S(2)}, u32[]{:S(2)}) collective-permute-start(f32[6,128]{1,0:T(8,128)S(1)} %get-tuple-element.126), channel_id=1, source_target_pairs={{7,0},{8,1},{9,2},{10,3},{11,4},{12,5},{13,6},{14,7},{15,8},{16,9}... | collective-permute-start | bytes 9224 | tf_op jit(solution)/shard_map/ppermute | solution.py:14
  291.9 53.9 %copy-start.59 = (s32[512,1]{0,1:T(1,128)S(1)}, s32[512,1]{0,1:T(1,128)}, u32[]{:S(2)}) copy-start(s32[512,1]{0,1:T(1,128)} %copy-done.58) | copy-start | bytes 6148
  298.2 47.3 %collective-permute-start.16 = (f32[6,128]{1,0:T(8,128)S(1)}, f32[6,128]{1,0:T(8,128)S(1)}, u32[]{:S(2)}, u32[]{:S(2)}) collective-permute-start(f32[6,128]{1,0:T(8,128)S(1)} %get-tuple-element.119), channel_id=1, source_target_pairs={{0,1},{1,2},{2,3},{3,4},{4,5},{5,6},{6,7},{7,8},{8,9},{9,10},{10,1... | collective-permute-start | bytes 9224 | tf_op jit(solution)/shard_map/ppermute | solution.py:14
  302.1 43.5 %collective-permute-start.17 = (f32[6,128]{1,0:T(8,128)S(1)}, f32[6,128]{1,0:T(8,128)S(1)}, u32[]{:S(2)}, u32[]{:S(2)}) collective-permute-start(f32[6,128]{1,0:T(8,128)S(1)} %get-tuple-element.122), channel_id=1, source_target_pairs={{0,9},{1,10},{2,11},{3,12},{4,13},{5,14},{6,15},{7,16},{8,17},{9,1... | collective-permute-start | bytes 9224 | tf_op jit(solution)/shard_map/ppermute | solution.py:14
  303.4 42.2 %collective-permute-start.18 = (f32[6,128]{1,0:T(8,128)S(1)}, f32[6,128]{1,0:T(8,128)S(1)}, u32[]{:S(2)}, u32[]{:S(2)}) collective-permute-start(f32[6,128]{1,0:T(8,128)S(1)} %get-tuple-element.121), channel_id=1, source_target_pairs={{0,8},{1,9},{2,10},{3,11},{4,12},{5,13},{6,14},{7,15},{8,16},{9,17... | collective-permute-start | bytes 9224 | tf_op jit(solution)/shard_map/ppermute | solution.py:14
  306.5 39.1 %collective-permute-start.19 = (f32[6,128]{1,0:T(8,128)S(1)}, f32[6,128]{1,0:T(8,128)S(1)}, u32[]{:S(2)}, u32[]{:S(2)}) collective-permute-start(f32[6,128]{1,0:T(8,128)S(1)} %get-tuple-element.120), channel_id=1, source_target_pairs={{0,7},{1,8},{2,9},{3,10},{4,11},{5,12},{6,13},{7,14},{8,15},{9,16}... | collective-permute-start | bytes 9224 | tf_op jit(solution)/shard_map/ppermute | solution.py:14
  351.4 39.6 %copy-start.37 = (s32[1024]{0:T(1024)S(1)}, s32[1024]{0:T(1024)}, u32[]{:S(2)}) copy-start(s32[1024]{0:T(1024)} %broadcast_clamp_fusion) | copy-start | bytes 12292
  373.5 112.4 %copy-start.50 = (f32[1,2560]{1,0:T(1,128)S(1)}, f32[1,2560]{1,0:T(1,128)}, u32[]{:S(2)}) copy-start(f32[1,2560]{1,0:T(1,128)} %get-tuple-element.61) | copy-start | bytes 30724
  373.5 112.4 %copy-start.55 = (f32[1,2560]{1,0:T(1,128)S(1)}, f32[1,2560]{1,0:T(1,128)}, u32[]{:S(2)}) copy-start(f32[1,2560]{1,0:T(1,128)} %get-tuple-element.62) | copy-start | bytes 30724
  375.9 110.2 %copy-start.66 = (f32[1,4,256]{2,1,0:T(4,128)S(1)}, f32[1,4,256]{2,1,0:T(4,128)}, u32[]{:S(2)}) copy-start(f32[1,4,256]{2,1,0:T(4,128)} %sub.334) | copy-start | bytes 12292
  375.9 110.2 %copy-start.67 = (f32[1,4,256]{2,1,0:T(4,128)S(1)}, f32[1,4,256]{2,1,0:T(4,128)}, u32[]{:S(2)}) copy-start(f32[1,4,256]{2,1,0:T(4,128)} %sqrt.64) | copy-start | bytes 12292
  376.0 110.2 %copy-start.68 = (f32[1,4,256]{2,1,0:T(4,128)S(1)}, f32[1,4,256]{2,1,0:T(4,128)}, u32[]{:S(2)}) copy-start(f32[1,4,256]{2,1,0:T(4,128)} %squeeze.193) | copy-start | bytes 12292
  376.0 110.2 %copy-start.69 = (f32[1,4,256]{2,1,0:T(4,128)S(1)}, f32[1,4,256]{2,1,0:T(4,128)}, u32[]{:S(2)}) copy-start(f32[1,4,256]{2,1,0:T(4,128)} %squeeze.194) | copy-start | bytes 12292
  376.0 110.2 %copy-start.77 = (s32[1,4]{1,0:T(1,128)S(1)}, s32[1,4]{1,0:T(1,128)}, u32[]{:S(2)}) copy-start(s32[1,4]{1,0:T(1,128)} %param.40) | copy-start | bytes 52
  376.3 9.5 %collective-permute-start.20 = (f32[6,128]{1,0:T(8,128)S(1)}, f32[6,128]{1,0:T(8,128)S(1)}, u32[]{:S(2)}, u32[]{:S(2)}) collective-permute-start(f32[6,128]{1,0:T(8,128)S(1)} %get-tuple-element.115), channel_id=1, source_target_pairs={{1,0},{2,1},{3,2},{4,3},{5,4},{6,5},{7,6},{8,7},{9,8},{10,9},{11,1... | collective-permute-start | bytes 9224 | tf_op jit(solution)/shard_map/ppermute | solution.py:14
  381.3 5.8 %collective-permute-start.21 = (f32[6,128]{1,0:T(8,128)S(1)}, f32[6,128]{1,0:T(8,128)S(1)}, u32[]{:S(2)}, u32[]{:S(2)}) collective-permute-start(f32[6,128]{1,0:T(8,128)S(1)} %get-tuple-element.118), channel_id=1, source_target_pairs={{9,0},{10,1},{11,2},{12,3},{13,4},{14,5},{15,6},{16,7},{17,8},{18,... | collective-permute-start | bytes 9224 | tf_op jit(solution)/shard_map/ppermute | solution.py:14
  382.6 4.5 collective-permute-start.22
  383.9 6.9 %collective-permute-start.23 = (f32[6,128]{1,0:T(8,128)S(1)}, f32[6,128]{1,0:T(8,128)S(1)}, u32[]{:S(2)}, u32[]{:S(2)}) collective-permute-start(f32[6,128]{1,0:T(8,128)S(1)} %get-tuple-element.116), channel_id=1, source_target_pairs={{7,0},{8,1},{9,2},{10,3},{11,4},{12,5},{13,6},{14,7},{15,8},{16,9}... | collective-permute-start | bytes 9224 | tf_op jit(solution)/shard_map/ppermute | solution.py:14
  468.0 55.1 %copy-start.60 = (s32[512,1]{0,1:T(1,128)S(1)}, s32[512,1]{0,1:T(1,128)}, u32[]{:S(2)}) copy-start(s32[512,1]{0,1:T(1,128)} %copy-done.58) | copy-start | bytes 6148
  474.4 48.5 %collective-permute-start.24 = (f32[6,128]{1,0:T(8,128)S(1)}, f32[6,128]{1,0:T(8,128)S(1)}, u32[]{:S(2)}, u32[]{:S(2)}) collective-permute-start(f32[6,128]{1,0:T(8,128)S(1)} %get-tuple-element.109), channel_id=1, source_target_pairs={{0,1},{1,2},{2,3},{3,4},{4,5},{5,6},{6,7},{7,8},{8,9},{9,10},{10,1... | collective-permute-start | bytes 9224 | tf_op jit(solution)/shard_map/ppermute | solution.py:14
  476.3 46.5 %collective-permute-start.25 = (f32[6,128]{1,0:T(8,128)S(1)}, f32[6,128]{1,0:T(8,128)S(1)}, u32[]{:S(2)}, u32[]{:S(2)}) collective-permute-start(f32[6,128]{1,0:T(8,128)S(1)} %get-tuple-element.112), channel_id=1, source_target_pairs={{0,9},{1,10},{2,11},{3,12},{4,13},{5,14},{6,15},{7,16},{8,17},{9,1... | collective-permute-start | bytes 9224 | tf_op jit(solution)/shard_map/ppermute | solution.py:14
  478.7 44.2 %collective-permute-start.26 = (f32[6,128]{1,0:T(8,128)S(1)}, f32[6,128]{1,0:T(8,128)S(1)}, u32[]{:S(2)}, u32[]{:S(2)}) collective-permute-start(f32[6,128]{1,0:T(8,128)S(1)} %get-tuple-element.111), channel_id=1, source_target_pairs={{0,8},{1,9},{2,10},{3,11},{4,12},{5,13},{6,14},{7,15},{8,16},{9,17... | collective-permute-start | bytes 9224 | tf_op jit(solution)/shard_map/ppermute | solution.py:14
  480.9 42.0 %collective-permute-start.27 = (f32[6,128]{1,0:T(8,128)S(1)}, f32[6,128]{1,0:T(8,128)S(1)}, u32[]{:S(2)}, u32[]{:S(2)}) collective-permute-start(f32[6,128]{1,0:T(8,128)S(1)} %get-tuple-element.110), channel_id=1, source_target_pairs={{0,7},{1,8},{2,9},{3,10},{4,11},{5,12},{6,13},{7,14},{8,15},{9,16}... | collective-permute-start | bytes 9224 | tf_op jit(solution)/shard_map/ppermute | solution.py:14
  (58 other events, 1008.9 us)
where the time goes:
time: 539 us; the launch traced here: 529 us
  other arithmetic  154 us (29%)
  blocking collectives  143 us (27%)
  local copies, waits for them, and re-layouts  138 us (26%)
  starting transfers between devices  71.9 us (13%)
  waiting for transfers between devices  11.1 us (2%)
  between operations  10.8 us (2%)
    psum x2, blocking collectives, sum_pairs(): return lax.psum((first_term, second_term), ('gx', 'gy'))  143 us
    scatter-add x3, other arithmetic, spread(): loads = jnp.zeros((6, seg_rows), jnp.float32).at[:, all_rows].add(pushes)  101 us
    gather x8, local copies, waits for them, and re-layouts, picked(): taken = jnp.take(source, all_rows, axis=1)  91.8 us
    ppermute x28, starting transfers between devices, passed_along(): return lax.ppermute(shard, axis, pairs)  71.9 us
    scatter-add x3, other arithmetic, spread(): jnp.zeros((6, 4 * export_cap), jnp.float32).at[:, slot_flat].add(cross_two)  18.5 us
    gather x8, local copies, waits for them, and re-layouts, incoming(): return jnp.take(flattened, slot_flat, axis=1)  12.5 us
    scatter-add x3, other arithmetic, spread(): loads.at[:, export_flat].add(jnp.moveaxis(returned, 0, 1).reshape(6, -1))  11.9 us
    ppermute x28, waiting for transfers between devices, passed_along(): return lax.ppermute(shard, axis, pairs)  11.1 us
  transfers between devices with their start and end apart: 28, of which 5 were waited for; matrix products, arithmetic and copies ran while one was open for 35% of the time, Pallas kernels for 0%

commit v1 on v0

--- a/solution.py
+++ b/solution.py
@@ -6,6 +6,7 @@
 step_time = 0.5
 floor_gap = 0.25
 tiny = 1e-06
+apply_panels = lambda row_data: jax.lax.psum(jax.lax.psum(row_data, "gy"), "gx")
 
 
 def passed_along(shard, axis, by):
@@ -77,7 +78,7 @@
 
 
 def sum_pairs(first_term, second_term):
-    return lax.psum((first_term, second_term), ("gx", "gy"))
+    return apply_panels((first_term, second_term))
 
 
 def on_device(

time: 539 us -> 497 us (0.922); the launches traced: 529 us -> 494 us
  blocking collectives: 143 us -> 105 us
    psum x2 -> x4, blocking collectives: 143 us -> 105 us  [the longest x2 81.7 us: jax.lax.psum(jax.lax.psum(row_data, 'gy'), 'gx')]
  transfers between devices with their start and end apart: 28 -> 28, of which waited for: 5 -> 5; matrix products, arithmetic and copies ran while one was open for 35% -> 37% of each run, Pallas kernels for 0% -> 0%
where the time goes in v1:
time: 497 us; the launch traced here: 494 us
  other arithmetic  154 us (31%)
  local copies, waits for them, and re-layouts  138 us (28%)
  blocking collectives  105 us (21%)
  starting transfers between devices  76.3 us (15%)
  between operations  10.6 us (2%)
  waiting for transfers between devices  9.83 us (2%)
    scatter-add x3, other arithmetic, spread(): loads = jnp.zeros((6, seg_rows), jnp.float32).at[:, all_rows].add(pushes)  101 us
    gather x8, local copies, waits for them, and re-layouts, picked(): taken = jnp.take(source, all_rows, axis=1)  91.8 us
    psum x2, blocking collectives, jax.lax.psum(jax.lax.psum(row_data, 'gy'), 'gx')  81.7 us
    ppermute x28, starting transfers between devices, passed_along(): return lax.ppermute(shard, axis, pairs)  76.3 us
    psum x2, blocking collectives, jax.lax.psum(row_data, 'gy')  23.2 us
    scatter-add x3, other arithmetic, spread(): jnp.zeros((6, 4 * export_cap), jnp.float32).at[:, slot_flat].add(cross_two)  18.5 us
    gather x8, local copies, waits for them, and re-layouts, incoming(): return jnp.take(flattened, slot_flat, axis=1)  12.5 us
    scatter-add x3, other arithmetic, spread(): loads.at[:, export_flat].add(jnp.moveaxis(returned, 0, 1).reshape(6, -1))  11.7 us
  transfers between devices with their start and end apart: 28, of which 5 were waited for; matrix products, arithmetic and copies ran while one was open for 37% of the time, Pallas kernels for 0%

profile of v1, /device:TPU:1, one launch (start us, length us, event | category | flops | bytes accessed | tf_op | source)
XLA Modules:
  0.0 493.5 jit_solution(9852824434111863647)
XLA Ops:
  11.4 3.3 collective-permute-start
  14.7 1.3 collective-permute-start.1
  16.0 1.3 collective-permute-start.2
  17.3 1.3 collective-permute-start.3
  19.2 1.9 collective-permute-start.4
  23.0 20.9 %gather_fusion.1 = f32[6144,6]{1,0:T(8,128)} fusion(f32[6,2048]{0,1:T(8,128)S(1)} %copy.319, s32[6144]{0:T(1024)S(1)} %fusion.33), kind=kCustom, calls=%fused_computation.3.clone | custom fusion | bytes 319488 | tf_op jit(solution)/shard_map/jit(_take)/gather | solution.py:122
  43.9 20.9 %gather_fusion = f32[6144,6]{1,0:T(8,128)} fusion(f32[6,2048]{0,1:T(8,128)S(1)} %copy.317, s32[6144]{0:T(1024)S(1)} %fusion.33), kind=kCustom, calls=%fused_computation.clone | custom fusion | bytes 319488 | tf_op jit(solution)/shard_map/jit(_take)/gather | solution.py:122
  66.0 2.4 copy.320
  72.4 1.9 slice_reduce_fusion.1
  75.3 1.3 reshape_dynamic-update-slice_fusion
  88.5 3.3 gather_fusion.3
  92.7 1.6 collective-permute-done.7
  94.6 2.8 gather_fusion.5
  100.2 6.1 %scatter_custom_fusion.1 = f32[6,512]{0,1:T(8,128)S(1)} fusion(s32[1024]{0:T(1024)S(1)} %bitcast.296, f32[1024,6]{1,0:T(8,128)S(1)} %copy.336, f32[]{:T(128)} %constant.32.clone.1), kind=kCustom, calls=%fused_computation.39 | custom fusion | flops 6144 | bytes 12292 | tf_op jit(solution)/shard_map/scatter-add | solution.py:154
  106.4 4.1 collective-permute-start.8
  110.4 5.0 %collective-permute-start.9 = (f32[6,128]{1,0:T(8,128)S(1)}, f32[6,128]{1,0:T(8,128)S(1)}, u32[]{:S(2)}, u32[]{:S(2)}) collective-permute-start(f32[6,128]{1,0:T(8,128)S(1)} %get-tuple-element.136), channel_id=1, source_target_pairs={{0,9},{1,10},{2,11},{3,12},{4,13},{5,14},{6,15},{7,16},{8,17},{9,1... | collective-permute-start | bytes 9224 | tf_op jit(solution)/shard_map/ppermute | solution.py:15
  115.5 5.1 %collective-permute-start.10 = (f32[6,128]{1,0:T(8,128)S(1)}, f32[6,128]{1,0:T(8,128)S(1)}, u32[]{:S(2)}, u32[]{:S(2)}) collective-permute-start(f32[6,128]{1,0:T(8,128)S(1)} %get-tuple-element.135), channel_id=1, source_target_pairs={{0,8},{1,9},{2,10},{3,11},{4,12},{5,13},{6,14},{7,15},{8,16},{9,17... | collective-permute-start | bytes 9224 | tf_op jit(solution)/shard_map/ppermute | solution.py:15
  120.6 6.2 %collective-permute-start.11 = (f32[6,128]{1,0:T(8,128)S(1)}, f32[6,128]{1,0:T(8,128)S(1)}, u32[]{:S(2)}, u32[]{:S(2)}) collective-permute-start(f32[6,128]{1,0:T(8,128)S(1)} %get-tuple-element.134), channel_id=1, source_target_pairs={{0,7},{1,8},{2,9},{3,10},{4,11},{5,12},{6,13},{7,14},{8,15},{9,16}... | collective-permute-start | bytes 9224 | tf_op jit(solution)/shard_map/ppermute | solution.py:15
  128.0 2.2 copy.335
  130.8 33.7 %scatter_custom_fusion = f32[6,2048]{0,1:T(8,128)S(1)} fusion(s32[6144]{0:T(1024)S(1)} %bitcast.275, f32[6144,6]{1,0:T(8,128)} %copy.335, f32[]{:T(128)} %constant.32.clone.1), kind=kCustom, calls=%fused_computation.25 | custom fusion | flops 36864 | bytes 49664 | tf_op jit(solution)/shard_map/scatter-add | solution.py:157
  164.9 3.9 scatter_fusion
  171.5 20.9 %gather_fusion.6 = f32[6144,6]{1,0:T(8,128)} fusion(f32[6,2048]{0,1:T(8,128)S(1)} %copy.344, s32[6144]{0:T(1024)S(1)} %copy-done.4), kind=kCustom, calls=%fused_computation.4.clone | custom fusion | bytes 319488 | tf_op jit(solution)/shard_map/jit(_take)/gather | solution.py:122
  192.6 3.2 collective-permute-start.12
  199.7 2.4 copy.345
  204.0 4.1 collective-permute-done.15
  208.3 2.8 gather_fusion.8
  215.3 11.1 %all-reduce.3 = (f32[]{:T(128)}, f32[]{:T(128)}) all-reduce(f32[]{:T(128)S(6)} %add.318, f32[]{:T(128)S(6)} %add.327), channel_id=1, replica_groups=mesh['gx'=16,'gy'=8] {'gy'}, use_global_device_ids=true, to_apply=%region_11.15 | all-reduce | flops 2 | bytes 16 | tf_op jit(solution)/shard_map/psum | solution.py:9
  226.4 43.8 %all-reduce.1 = (f32[]{:T(128)}, f32[]{:T(128)}) all-reduce(f32[]{:T(128)} %get-tuple-element.52, f32[]{:T(128)} %get-tuple-element.53), channel_id=1, replica_groups=mesh['gx'=16,'gy'=8] {'gx'}, use_global_device_ids=true, to_apply=%region_12.16 | all-reduce | flops 2 | bytes 16 | tf_op jit(solution)/shard_map/psum | solution.py:9
  271.8 6.2 %scatter_custom_fusion.4 = f32[6,512]{0,1:T(8,128)S(1)} fusion(s32[1024]{0:T(1024)} %bitcast.297, f32[1024,6]{1,0:T(8,128)S(1)} %copy.354, f32[]{:T(128)} %constant.32.clone.1), kind=kCustom, calls=%fused_computation.37 | custom fusion | flops 6144 | bytes 12800 | tf_op jit(solution)/shard_map/scatter-add | solution.py:154
  278.1 7.8 %collective-permute-start.16 = (f32[6,128]{1,0:T(8,128)S(1)}, f32[6,128]{1,0:T(8,128)S(1)}, u32[]{:S(2)}, u32[]{:S(2)}) collective-permute-start(f32[6,128]{1,0:T(8,128)S(1)} %get-tuple-element.123), channel_id=1, source_target_pairs={{0,1},{1,2},{2,3},{3,4},{4,5},{5,6},{6,7},{7,8},{8,9},{9,10},{10,1... | collective-permute-start | bytes 9224 | tf_op jit(solution)/shard_map/ppermute | solution.py:15
  288.5 3.3 collective-permute-start.19
  292.1 2.2 copy.353
  294.3 33.7 %scatter_custom_fusion.3 = f32[6,2048]{0,1:T(8,128)S(1)} fusion(s32[6144]{0:T(1024)} %bitcast.276, f32[6144,6]{1,0:T(8,128)} %copy.353, f32[]{:T(128)} %constant.32.clone.1), kind=kCustom, calls=%fused_computation.23 | custom fusion | flops 36864 | bytes 49664 | tf_op jit(solution)/shard_map/scatter-add | solution.py:157
  328.3 3.9 scatter_fusion.1
  333.9 20.9 %gather_fusion.9 = f32[6144,6]{1,0:T(8,128)} fusion(f32[6,2048]{0,1:T(8,128)S(1)} %copy.362, s32[6144]{0:T(1024)S(1)} %copy-done.4), kind=kCustom, calls=%fused_computation.5.clone | custom fusion | bytes 319488 | tf_op jit(solution)/shard_map/jit(_take)/gather | solution.py:122
  356.1 2.4 copy.363
  358.9 4.4 collective-permute-start.20
  369.1 2.5 collective-permute-done.23
  371.8 2.8 gather_fusion.11
  378.2 12.1 %all-reduce.2 = (f32[]{:T(128)}, f32[]{:T(128)}) all-reduce(f32[]{:T(128)S(6)} %add.329, f32[]{:T(128)S(6)} %add.336), channel_id=1, replica_groups=mesh['gx'=16,'gy'=8] {'gy'}, use_global_device_ids=true, to_apply=%region_29.33 | all-reduce | flops 2 | bytes 16 | tf_op jit(solution)/shard_map/psum | solution.py:9
  390.3 37.9 %all-reduce = (f32[]{:T(128)}, f32[]{:T(128)}) all-reduce(f32[]{:T(128)} %get-tuple-element.50, f32[]{:T(128)} %get-tuple-element.51), channel_id=1, replica_groups=mesh['gx'=16,'gy'=8] {'gx'}, use_global_device_ids=true, to_apply=%region_30.34 | all-reduce | flops 2 | bytes 16 | tf_op jit(solution)/shard_map/psum | solution.py:9
  430.4 6.2 %scatter_custom_fusion.7 = f32[6,512]{0,1:T(8,128)S(1)} fusion(s32[1024]{0:T(1024)} %bitcast.298, f32[1024,6]{1,0:T(8,128)S(1)} %copy.372, f32[]{:T(128)} %constant.32.clone.1), kind=kCustom, calls=%fused_computation.35 | custom fusion | flops 6144 | bytes 12800 | tf_op jit(solution)/shard_map/scatter-add | solution.py:154
  436.7 8.0 %collective-permute-start.24 = (f32[6,128]{1,0:T(8,128)S(1)}, f32[6,128]{1,0:T(8,128)S(1)}, u32[]{:S(2)}, u32[]{:S(2)}) collective-permute-start(f32[6,128]{1,0:T(8,128)S(1)} %get-tuple-element.113), channel_id=1, source_target_pairs={{0,1},{1,2},{2,3},{3,4},{4,5},{5,6},{6,7},{7,8},{8,9},{9,10},{10,1... | collective-permute-start | bytes 9224 | tf_op jit(solution)/shard_map/ppermute | solution.py:15
  446.0 2.0 collective-permute-start.26
  447.9 2.6 collective-permute-start.27
  451.5 2.2 copy.371
  453.7 33.7 %scatter_custom_fusion.6 = f32[6,2048]{0,1:T(8,128)S(1)} fusion(s32[6144]{0:T(1024)} %bitcast.277, f32[6144,6]{1,0:T(8,128)} %copy.371, f32[]{:T(128)} %constant.32.clone.1), kind=kCustom, calls=%fused_computation.21 | custom fusion | flops 36864 | bytes 49664 | tf_op jit(solution)/shard_map/scatter-add | solution.py:157
  487.8 4.0 scatter_fusion.2
  (381 shorter events, 65.4 us)
Async XLA Ops:
  2.1 62.7 %copy-start.73 = (pred[4,128]{1,0:T(4,128)(4,1)}, pred[4,128]{1,0:T(4,128)(4,1)S(1)}, u32[]{:S(2)}) copy-start(pred[4,128]{1,0:T(4,128)(4,1)S(1)} %compare_and_fusion.2) | copy-start | bytes 1540
  7.2 58.2 %copy-start.56 = (s32[1024]{0:T(1024)}, s32[1024]{0:T(1024)S(1)}, u32[]{:S(2)}) copy-start(s32[1024]{0:T(1024)S(1)} %pad_clamp_fusion) | copy-start | bytes 12292
  11.4 70.4 %collective-permute-start = (f32[6,128]{1,0:T(8,128)}, f32[6,128]{1,0:T(8,128)}, u32[]{:S(2)}, u32[]{:S(2)}) collective-permute-start(f32[6,128]{1,0:T(8,128)} %get-tuple-element.145), channel_id=1, source_target_pairs={{1,0},{2,1},{3,2},{4,3},{5,4},{6,5},{7,6},{8,7},{9,8},{10,9},{11,1... | collective-permute-start | bytes 9224 | tf_op jit(solution)/shard_map/ppermute | solution.py:15
  14.7 69.1 %collective-permute-start.1 = (f32[6,128]{1,0:T(8,128)}, f32[6,128]{1,0:T(8,128)}, u32[]{:S(2)}, u32[]{:S(2)}) collective-permute-start(f32[6,128]{1,0:T(8,128)} %get-tuple-element.148), channel_id=1, source_target_pairs={{9,0},{10,1},{11,2},{12,3},{13,4},{14,5},{15,6},{16,7},{17,8},{18,... | collective-permute-start | bytes 9224 | tf_op jit(solution)/shard_map/ppermute | solution.py:15
  16.0 69.7 %collective-permute-start.2 = (f32[6,128]{1,0:T(8,128)}, f32[6,128]{1,0:T(8,128)}, u32[]{:S(2)}, u32[]{:S(2)}) collective-permute-start(f32[6,128]{1,0:T(8,128)} %get-tuple-element.147), channel_id=1, source_target_pairs={{8,0},{9,1},{10,2},{11,3},{12,4},{13,5},{14,6},{15,7},{16,8},{17,9... | collective-permute-start | bytes 9224 | tf_op jit(solution)/shard_map/ppermute | solution.py:15
  17.3 70.4 %collective-permute-start.3 = (f32[6,128]{1,0:T(8,128)}, f32[6,128]{1,0:T(8,128)}, u32[]{:S(2)}, u32[]{:S(2)}) collective-permute-start(f32[6,128]{1,0:T(8,128)} %get-tuple-element.146), channel_id=1, source_target_pairs={{7,0},{8,1},{9,2},{10,3},{11,4},{12,5},{13,6},{14,7},{15,8},{16,9}... | collective-permute-start | bytes 9224 | tf_op jit(solution)/shard_map/ppermute | solution.py:15
  19.2 72.9 %collective-permute-start.4 = (f32[6,128]{1,0:T(8,128)}, f32[6,128]{1,0:T(8,128)}, u32[]{:S(2)}, u32[]{:S(2)}) collective-permute-start(f32[6,128]{1,0:T(8,128)} %get-tuple-element.141), channel_id=1, source_target_pairs={{1,0},{2,1},{3,2},{4,3},{5,4},{6,5},{7,6},{8,7},{9,8},{10,9},{11,1... | collective-permute-start | bytes 9224 | tf_op jit(solution)/shard_map/ppermute | solution.py:15
  78.7 52.1 %copy-start.61 = (s32[6144,1]{0,1:T(1,128)}, s32[6144,1]{0,1:T(1,128)S(1)}, u32[]{:S(2)}) copy-start(s32[6144,1]{0,1:T(1,128)S(1)} %compare_select_fusion) | copy-start | bytes 73732
  78.7 51.5 %copy-start.76 = (s32[1024,1]{0,1:T(1,128)}, s32[1024,1]{0,1:T(1,128)S(1)}, u32[]{:S(2)}) copy-start(s32[1024,1]{0,1:T(1,128)S(1)} %compare_select_fusion.2) | copy-start | bytes 12292
  80.3 84.6 %copy-start.58 = (s32[512,1]{0,1:T(1,128)}, s32[512,1]{0,1:T(1,128)S(1)}, u32[]{:S(2)}) copy-start(s32[512,1]{0,1:T(1,128)S(1)} %compare_select_fusion.3) | copy-start | bytes 6148
  81.7 48.5 %copy-start.38 = (f32[1,2,4,128]{3,1,2,0:T(2,128)}, f32[1,2,4,128]{3,1,2,0:T(2,128)S(1)}, u32[]{:S(2)}) copy-start(f32[1,2,4,128]{3,1,2,0:T(2,128)S(1)} %copy.396) | copy-start | bytes 12292
  81.7 11.0 %collective-permute-start.5 = (f32[6,128]{1,0:T(8,128)}, f32[6,128]{1,0:T(8,128)S(1)}, u32[]{:S(2)}, u32[]{:S(2)}) collective-permute-start(f32[6,128]{1,0:T(8,128)} %get-tuple-element.144), channel_id=1, source_target_pairs={{9,0},{10,1},{11,2},{12,3},{13,4},{14,5},{15,6},{16,7},{17,8},{18,... | collective-permute-start | bytes 9224 | tf_op jit(solution)/shard_map/ppermute | solution.py:15
  83.7 9.0 %collective-permute-start.6 = (f32[6,128]{1,0:T(8,128)}, f32[6,128]{1,0:T(8,128)S(1)}, u32[]{:S(2)}, u32[]{:S(2)}) collective-permute-start(f32[6,128]{1,0:T(8,128)} %get-tuple-element.143), channel_id=1, source_target_pairs={{8,0},{9,1},{10,2},{11,3},{12,4},{13,5},{14,6},{15,7},{16,8},{17,9... | collective-permute-start | bytes 9224 | tf_op jit(solution)/shard_map/ppermute | solution.py:15
  85.7 8.7 %collective-permute-start.7 = (f32[6,128]{1,0:T(8,128)}, f32[6,128]{1,0:T(8,128)S(1)}, u32[]{:S(2)}, u32[]{:S(2)}) collective-permute-start(f32[6,128]{1,0:T(8,128)} %get-tuple-element.142), channel_id=1, source_target_pairs={{7,0},{8,1},{9,2},{10,3},{11,4},{12,5},{13,6},{14,7},{15,8},{16,9}... | collective-permute-start | bytes 9224 | tf_op jit(solution)/shard_map/ppermute | solution.py:15
  98.8 65.8 %copy-start.9 = (f32[1,1024]{1,0:T(1,128)}, f32[1,1024]{1,0:T(1,128)S(1)}, u32[]{:S(2)}) copy-start(f32[1,1024]{1,0:T(1,128)S(1)} %get-tuple-element.110) | copy-start | bytes 12292
  98.8 65.8 %copy-start.12 = (f32[1,1024]{1,0:T(1,128)}, f32[1,1024]{1,0:T(1,128)S(1)}, u32[]{:S(2)}) copy-start(f32[1,1024]{1,0:T(1,128)S(1)} %get-tuple-element.111) | copy-start | bytes 12292
  98.8 65.8 %copy-start.15 = (f32[1,1024]{1,0:T(1,128)}, f32[1,1024]{1,0:T(1,128)S(1)}, u32[]{:S(2)}) copy-start(f32[1,1024]{1,0:T(1,128)S(1)} %get-tuple-element.112) | copy-start | bytes 12292
  106.4 58.2 %collective-permute-start.8 = (f32[6,128]{1,0:T(8,128)S(1)}, f32[6,128]{1,0:T(8,128)S(1)}, u32[]{:S(2)}, u32[]{:S(2)}) collective-permute-start(f32[6,128]{1,0:T(8,128)S(1)} %get-tuple-element.133), channel_id=1, source_target_pairs={{0,1},{1,2},{2,3},{3,4},{4,5},{5,6},{6,7},{7,8},{8,9},{9,10},{10,1... | collective-permute-start | bytes 9224 | tf_op jit(solution)/shard_map/ppermute | solution.py:15
  110.4 54.2 %collective-permute-start.9 = (f32[6,128]{1,0:T(8,128)S(1)}, f32[6,128]{1,0:T(8,128)S(1)}, u32[]{:S(2)}, u32[]{:S(2)}) collective-permute-start(f32[6,128]{1,0:T(8,128)S(1)} %get-tuple-element.136), channel_id=1, source_target_pairs={{0,9},{1,10},{2,11},{3,12},{4,13},{5,14},{6,15},{7,16},{8,17},{9,1... | collective-permute-start | bytes 9224 | tf_op jit(solution)/shard_map/ppermute | solution.py:15
  115.5 49.2 %collective-permute-start.10 = (f32[6,128]{1,0:T(8,128)S(1)}, f32[6,128]{1,0:T(8,128)S(1)}, u32[]{:S(2)}, u32[]{:S(2)}) collective-permute-start(f32[6,128]{1,0:T(8,128)S(1)} %get-tuple-element.135), channel_id=1, source_target_pairs={{0,8},{1,9},{2,10},{3,11},{4,12},{5,13},{6,14},{7,15},{8,16},{9,17... | collective-permute-start | bytes 9224 | tf_op jit(solution)/shard_map/ppermute | solution.py:15
  120.6 44.1 %collective-permute-start.11 = (f32[6,128]{1,0:T(8,128)S(1)}, f32[6,128]{1,0:T(8,128)S(1)}, u32[]{:S(2)}, u32[]{:S(2)}) collective-permute-start(f32[6,128]{1,0:T(8,128)S(1)} %get-tuple-element.134), channel_id=1, source_target_pairs={{0,7},{1,8},{2,9},{3,10},{4,11},{5,12},{6,13},{7,14},{8,15},{9,16}... | collective-permute-start | bytes 9224 | tf_op jit(solution)/shard_map/ppermute | solution.py:15
  192.6 11.0 %collective-permute-start.12 = (f32[6,128]{1,0:T(8,128)S(1)}, f32[6,128]{1,0:T(8,128)S(1)}, u32[]{:S(2)}, u32[]{:S(2)}) collective-permute-start(f32[6,128]{1,0:T(8,128)S(1)} %get-tuple-element.129), channel_id=1, source_target_pairs={{1,0},{2,1},{3,2},{4,3},{5,4},{6,5},{7,6},{8,7},{9,8},{10,9},{11,1... | collective-permute-start | bytes 9224 | tf_op jit(solution)/shard_map/ppermute | solution.py:15
  195.8 7.8 %collective-permute-start.13 = (f32[6,128]{1,0:T(8,128)S(1)}, f32[6,128]{1,0:T(8,128)S(1)}, u32[]{:S(2)}, u32[]{:S(2)}) collective-permute-start(f32[6,128]{1,0:T(8,128)S(1)} %get-tuple-element.132), channel_id=1, source_target_pairs={{9,0},{10,1},{11,2},{12,3},{13,4},{14,5},{15,6},{16,7},{17,8},{18,... | collective-permute-start | bytes 9224 | tf_op jit(solution)/shard_map/ppermute | solution.py:15
  197.1 6.9 %collective-permute-start.14 = (f32[6,128]{1,0:T(8,128)S(1)}, f32[6,128]{1,0:T(8,128)S(1)}, u32[]{:S(2)}, u32[]{:S(2)}) collective-permute-start(f32[6,128]{1,0:T(8,128)S(1)} %get-tuple-element.131), channel_id=1, source_target_pairs={{8,0},{9,1},{10,2},{11,3},{12,4},{13,5},{14,6},{15,7},{16,8},{17,9... | collective-permute-start | bytes 9224 | tf_op jit(solution)/shard_map/ppermute | solution.py:15
  198.4 93.4 %copy-start.49 = (f32[1,2560]{1,0:T(1,128)S(1)}, f32[1,2560]{1,0:T(1,128)}, u32[]{:S(2)}) copy-start(f32[1,2560]{1,0:T(1,128)} %get-tuple-element.65) | copy-start | bytes 30724
  198.4 9.7 %collective-permute-start.15 = (f32[6,128]{1,0:T(8,128)S(1)}, f32[6,128]{1,0:T(8,128)S(1)}, u32[]{:S(2)}, u32[]{:S(2)}) collective-permute-start(f32[6,128]{1,0:T(8,128)S(1)} %get-tuple-element.130), channel_id=1, source_target_pairs={{7,0},{8,1},{9,2},{10,3},{11,4},{12,5},{13,6},{14,7},{15,8},{16,9}... | collective-permute-start | bytes 9224 | tf_op jit(solution)/shard_map/ppermute | solution.py:15
  271.8 56.5 %copy-start.59 = (s32[512,1]{0,1:T(1,128)S(1)}, s32[512,1]{0,1:T(1,128)}, u32[]{:S(2)}) copy-start(s32[512,1]{0,1:T(1,128)} %copy-done.58) | copy-start | bytes 6148
  278.1 49.9 %collective-permute-start.16 = (f32[6,128]{1,0:T(8,128)S(1)}, f32[6,128]{1,0:T(8,128)S(1)}, u32[]{:S(2)}, u32[]{:S(2)}) collective-permute-start(f32[6,128]{1,0:T(8,128)S(1)} %get-tuple-element.123), channel_id=1, source_target_pairs={{0,1},{1,2},{2,3},{3,4},{4,5},{5,6},{6,7},{7,8},{8,9},{9,10},{10,1... | collective-permute-start | bytes 9224 | tf_op jit(solution)/shard_map/ppermute | solution.py:15
  285.9 42.1 %collective-permute-start.17 = (f32[6,128]{1,0:T(8,128)S(1)}, f32[6,128]{1,0:T(8,128)S(1)}, u32[]{:S(2)}, u32[]{:S(2)}) collective-permute-start(f32[6,128]{1,0:T(8,128)S(1)} %get-tuple-element.126), channel_id=1, source_target_pairs={{0,9},{1,10},{2,11},{3,12},{4,13},{5,14},{6,15},{7,16},{8,17},{9,1... | collective-permute-start | bytes 9224 | tf_op jit(solution)/shard_map/ppermute | solution.py:15
  287.2 40.8 %collective-permute-start.18 = (f32[6,128]{1,0:T(8,128)S(1)}, f32[6,128]{1,0:T(8,128)S(1)}, u32[]{:S(2)}, u32[]{:S(2)}) collective-permute-start(f32[6,128]{1,0:T(8,128)S(1)} %get-tuple-element.125), channel_id=1, source_target_pairs={{0,8},{1,9},{2,10},{3,11},{4,12},{5,13},{6,14},{7,15},{8,16},{9,17... | collective-permute-start | bytes 9224 | tf_op jit(solution)/shard_map/ppermute | solution.py:15
  288.5 39.6 %collective-permute-start.19 = (f32[6,128]{1,0:T(8,128)S(1)}, f32[6,128]{1,0:T(8,128)S(1)}, u32[]{:S(2)}, u32[]{:S(2)}) collective-permute-start(f32[6,128]{1,0:T(8,128)S(1)} %get-tuple-element.124), channel_id=1, source_target_pairs={{0,7},{1,8},{2,9},{3,10},{4,11},{5,12},{6,13},{7,14},{8,15},{9,16}... | collective-permute-start | bytes 9224 | tf_op jit(solution)/shard_map/ppermute | solution.py:15
  333.9 37.8 %copy-start.37 = (s32[1024]{0:T(1024)S(1)}, s32[1024]{0:T(1024)}, u32[]{:S(2)}) copy-start(s32[1024]{0:T(1024)} %broadcast_clamp_fusion) | copy-start | bytes 12292
  356.1 94.5 %copy-start.50 = (f32[1,2560]{1,0:T(1,128)S(1)}, f32[1,2560]{1,0:T(1,128)}, u32[]{:S(2)}) copy-start(f32[1,2560]{1,0:T(1,128)} %get-tuple-element.65) | copy-start | bytes 30724
  356.1 94.5 %copy-start.55 = (f32[1,2560]{1,0:T(1,128)S(1)}, f32[1,2560]{1,0:T(1,128)}, u32[]{:S(2)}) copy-start(f32[1,2560]{1,0:T(1,128)} %get-tuple-element.66) | copy-start | bytes 30724
  358.5 92.3 %copy-start.66 = (f32[1,4,256]{2,1,0:T(4,128)S(1)}, f32[1,4,256]{2,1,0:T(4,128)}, u32[]{:S(2)}) copy-start(f32[1,4,256]{2,1,0:T(4,128)} %sub.334) | copy-start | bytes 12292
  358.5 92.3 %copy-start.67 = (f32[1,4,256]{2,1,0:T(4,128)S(1)}, f32[1,4,256]{2,1,0:T(4,128)}, u32[]{:S(2)}) copy-start(f32[1,4,256]{2,1,0:T(4,128)} %sqrt.64) | copy-start | bytes 12292
  358.5 92.3 %copy-start.68 = (f32[1,4,256]{2,1,0:T(4,128)S(1)}, f32[1,4,256]{2,1,0:T(4,128)}, u32[]{:S(2)}) copy-start(f32[1,4,256]{2,1,0:T(4,128)} %squeeze.193) | copy-start | bytes 12292
  358.5 92.3 %copy-start.69 = (f32[1,4,256]{2,1,0:T(4,128)S(1)}, f32[1,4,256]{2,1,0:T(4,128)}, u32[]{:S(2)}) copy-start(f32[1,4,256]{2,1,0:T(4,128)} %squeeze.194) | copy-start | bytes 12292
  358.5 92.3 %copy-start.77 = (s32[1,4]{1,0:T(1,128)S(1)}, s32[1,4]{1,0:T(1,128)}, u32[]{:S(2)}) copy-start(s32[1,4]{1,0:T(1,128)} %param.40) | copy-start | bytes 52
  358.9 9.0 %collective-permute-start.20 = (f32[6,128]{1,0:T(8,128)S(1)}, f32[6,128]{1,0:T(8,128)S(1)}, u32[]{:S(2)}, u32[]{:S(2)}) collective-permute-start(f32[6,128]{1,0:T(8,128)S(1)} %get-tuple-element.119), channel_id=1, source_target_pairs={{1,0},{2,1},{3,2},{4,3},{5,4},{6,5},{7,6},{8,7},{9,8},{10,9},{11,1... | collective-permute-start | bytes 9224 | tf_op jit(solution)/shard_map/ppermute | solution.py:15
  363.3 5.8 %collective-permute-start.21 = (f32[6,128]{1,0:T(8,128)S(1)}, f32[6,128]{1,0:T(8,128)S(1)}, u32[]{:S(2)}, u32[]{:S(2)}) collective-permute-start(f32[6,128]{1,0:T(8,128)S(1)} %get-tuple-element.122), channel_id=1, source_target_pairs={{9,0},{10,1},{11,2},{12,3},{13,4},{14,5},{15,6},{16,7},{17,8},{18,... | collective-permute-start | bytes 9224 | tf_op jit(solution)/shard_map/ppermute | solution.py:15
  364.6 4.5 collective-permute-start.22
  365.9 5.7 %collective-permute-start.23 = (f32[6,128]{1,0:T(8,128)S(1)}, f32[6,128]{1,0:T(8,128)S(1)}, u32[]{:S(2)}, u32[]{:S(2)}) collective-permute-start(f32[6,128]{1,0:T(8,128)S(1)} %get-tuple-element.120), channel_id=1, source_target_pairs={{7,0},{8,1},{9,2},{10,3},{11,4},{12,5},{13,6},{14,7},{15,8},{16,9}... | collective-permute-start | bytes 9224 | tf_op jit(solution)/shard_map/ppermute | solution.py:15
  430.4 57.4 %copy-start.60 = (s32[512,1]{0,1:T(1,128)S(1)}, s32[512,1]{0,1:T(1,128)}, u32[]{:S(2)}) copy-start(s32[512,1]{0,1:T(1,128)} %copy-done.58) | copy-start | bytes 6148
  436.7 50.8 %collective-permute-start.24 = (f32[6,128]{1,0:T(8,128)S(1)}, f32[6,128]{1,0:T(8,128)S(1)}, u32[]{:S(2)}, u32[]{:S(2)}) collective-permute-start(f32[6,128]{1,0:T(8,128)S(1)} %get-tuple-element.113), channel_id=1, source_target_pairs={{0,1},{1,2},{2,3},{3,4},{4,5},{5,6},{6,7},{7,8},{8,9},{9,10},{10,1... | collective-permute-start | bytes 9224 | tf_op jit(solution)/shard_map/ppermute | solution.py:15
  444.7 42.8 %collective-permute-start.25 = (f32[6,128]{1,0:T(8,128)S(1)}, f32[6,128]{1,0:T(8,128)S(1)}, u32[]{:S(2)}, u32[]{:S(2)}) collective-permute-start(f32[6,128]{1,0:T(8,128)S(1)} %get-tuple-element.116), channel_id=1, source_target_pairs={{0,9},{1,10},{2,11},{3,12},{4,13},{5,14},{6,15},{7,16},{8,17},{9,1... | collective-permute-start | bytes 9224 | tf_op jit(solution)/shard_map/ppermute | solution.py:15
  446.0 41.6 %collective-permute-start.26 = (f32[6,128]{1,0:T(8,128)S(1)}, f32[6,128]{1,0:T(8,128)S(1)}, u32[]{:S(2)}, u32[]{:S(2)}) collective-permute-start(f32[6,128]{1,0:T(8,128)S(1)} %get-tuple-element.115), channel_id=1, source_target_pairs={{0,8},{1,9},{2,10},{3,11},{4,12},{5,13},{6,14},{7,15},{8,16},{9,17... | collective-permute-start | bytes 9224 | tf_op jit(solution)/shard_map/ppermute | solution.py:15
  447.9 39.6 %collective-permute-start.27 = (f32[6,128]{1,0:T(8,128)S(1)}, f32[6,128]{1,0:T(8,128)S(1)}, u32[]{:S(2)}, u32[]{:S(2)}) collective-permute-start(f32[6,128]{1,0:T(8,128)S(1)} %get-tuple-element.114), channel_id=1, source_target_pairs={{0,7},{1,8},{2,9},{3,10},{4,11},{5,12},{6,13},{7,14},{8,15},{9,16}... | collective-permute-start | bytes 9224 | tf_op jit(solution)/shard_map/ppermute | solution.py:15
  (58 other events, 992.8 us)
